TPU v7x, 32 devices: a whole 2x2x4 slice. The times are simulated.
32 devices in a mesh: group: 4 (over x, core), dom: 8 (over z, y).
Axes of the slice: x: 2, y: 2, z: 4, core: 2. Of those that a mesh axis runs over, the one named last changes fastest.
Arguments:
- features: bfloat16 [16384, 512], P(('group', 'dom')), may hold values from -6 to 6
- w_query: bfloat16 [512, 512], replicated
- w_key: bfloat16 [512, 512], replicated
- w_value: bfloat16 [512, 512], replicated, may hold values from -0.25 to 0.25
- w_out: bfloat16 [512, 512], replicated, may hold values from -0.25 to 0.25
- w_up: bfloat16 [512, 2048], replicated, may hold values from -0.25 to 0.25
- w_down: bfloat16 [2048, 512], replicated, may hold values from -0.125 to 0.125
- block_len: int32 [128], P(('group', 'dom')), may hold values from 32 to 128, as said below
- cross_blocks: int32 [128, 2], P(('group', 'dom')), may hold values from 0 to 127, as said below
- cross_count: int32 [128], P(('group', 'dom')), may hold values from 1 to 2, as said below
Outputs:
- layer_out: bfloat16 [16384, 512], P(('group', 'dom'))
Inputs may be any that keep to these rules, and one draw needn't show every extreme that they name: `block_len`: block 0 has all 128 nodes live. Block cross_blocks[b, c] lies in a group other than b's, at the same index of dom as block b, that is cross_blocks[b, c] // 4 % 8 == b // 4 % 8. `cross_count`: block 0 uses all 2 listed key blocks.
All inputs are finite; a program needn't handle non-finite values.
Results may differ from a plain program's by a relative error of at most 0.012.
The roundings to bfloat16 on the way count: a program that leaves them out, or rounds other values in their place, can miss the bound.
Values may be sent and summed in bfloat16 or wider, within the bound.
No kernel may reach another device: no remote copies, remote signals or barrier semaphores. Data moves between devices by JAX's collectives and lax.ppermute only.
A program may use at most 320 MiB of HBM per device.

v0:
```python
import jax
import jax.numpy as jnp
from jax import lax
from jax.experimental import pallas as pl
from jax.experimental.pallas import tpu as pltpu
from jax.sharding import PartitionSpec as P


HEADS = 8
CROSS = 2
BF = jnp.bfloat16
F32 = jnp.float32
DEAD = 1e30
DEAD_FROM = 1e29
LOG2E = 1.4426950408889634
ONES = 16
NT = (((1,), (1,)), ((), ()))


def vmem():
    return pl.BlockSpec(memory_space=pltpu.VMEM)


def smem():
    return pl.BlockSpec(memory_space=pltpu.SMEM)


def hbm():
    return pl.BlockSpec(memory_space=pltpu.HBM)


def kernel_call(kernel, args, specs, outs, flops, scratch=(), aliases=None, limit=24):
    moved = sum(a.size * a.dtype.itemsize for a in args) + sum(
        o.size * o.dtype.itemsize for o in outs
    )
    return pl.pallas_call(
        kernel,
        out_shape=tuple(outs),
        in_specs=specs,
        out_specs=tuple(vmem() for _ in outs),
        scratch_shapes=list(scratch),
        input_output_aliases=aliases or {},
        compiler_params=pltpu.CompilerParams(vmem_limit_bytes=limit << 20),
        cost_estimate=pl.CostEstimate(flops=flops, bytes_accessed=moved, transcendentals=0),
    )(*args)


def normed_rows(wide):
    return wide * lax.rsqrt(jnp.mean(wide * wide, axis=-1, keepdims=True) + 1e-06)


def start_copies(pairs, sems):
    copies = [pltpu.make_async_copy(a, b, sems.at[i]) for i, (a, b) in enumerate(pairs)]
    for copy in copies:
        copy.start()
    return copies


def norm_kernel(len_hbm, feat_hbm, out_ref, len_ref, feat_ref, sems):
    rows, width = feat_ref.shape
    blocks = len_ref.shape[0]
    per = rows // blocks
    spans = [slice(b * per, (b + 1) * per) for b in range(blocks)]
    copies = start_copies(
        [(len_hbm, len_ref)] + [(feat_hbm.at[s], feat_ref.at[s]) for s in spans], sems
    )
    copies[0].wait()
    place = lax.broadcasted_iota(jnp.int32, (per, width), 0)
    for b, span in enumerate(spans):
        copies[b + 1].wait()
        row = normed_rows(feat_ref[span, :].astype(F32))
        out_ref[span, :] = jnp.where(place < len_ref[b], row, DEAD).astype(BF)


def prepare(x, spare, span, xk_ref, xv_ref, flag_ref):
    live = x[:, :1] < DEAD_FROM
    xk_ref[span, :] = jnp.where(live, x, spare).astype(BF)
    xv_ref[span, :] = jnp.where(live, x, 0.0).astype(BF)
    flag_ref[span, :] = jnp.broadcast_to(
        jnp.where(live, 1.0, 0.0), (x.shape[0], flag_ref.shape[1])
    ).astype(BF)


def keys_values(xk_ref, xv_ref, flag_ref, wk_ref, wvt_ref):
    keys = jnp.dot(xk_ref[...], wk_ref[...], preferred_element_type=F32).astype(BF)
    vals = lax.dot_general(wvt_ref[...], xv_ref[...], NT, preferred_element_type=F32).astype(BF)
    lane = lax.broadcasted_iota(jnp.int32, (ONES, flag_ref.shape[1]), 1)
    ones = lax.dot_general(
        jnp.where(lane == 0, 1.0, 0.0).astype(BF), flag_ref[...], NT, preferred_element_type=F32
    ).astype(BF)
    return keys, vals, ones


def attend(xs, qt_ref, wk_ref, wvt_ref, acc_ref, top_ref, first):
    keys, vals, ones = keys_values(*xs, wk_ref, wvt_ref)
    size = vals.shape[0] // HEADS
    for h in range(HEADS):
        pair = keys[:, h // 2 * 2 * size : (h // 2 + 1) * 2 * size]
        s = jnp.dot(
            jnp.concatenate([pair, pair], axis=1), qt_ref[h], preferred_element_type=F32
        )
        top = jnp.max(s, axis=0, keepdims=True)
        if not first:
            before = top_ref[h : h + 1, :]
            top = jnp.maximum(before, top)
        p = jnp.exp2(s - top).astype(BF)
        val = jnp.concatenate([vals[h * size : (h + 1) * size], ones], axis=0)
        added = jnp.dot(val, p, preferred_element_type=F32)
        if not first:
            added = acc_ref[h] * jnp.exp2(before - top) + added
        acc_ref[h] = added
        top_ref[h : h + 1, :] = top


def first_kernel(
    xs_ref, feat_hbm, wq_hbm, wk_hbm, wv_hbm, qt_ref, wk_ref, wvt_ref, acc_ref, top_ref,
    feat_ref, wq_ref, wv_ref, sems, xk_ref, xv_ref, flag_ref,
):
    copies = start_copies(
        [(feat_hbm, feat_ref), (wq_hbm, wq_ref), (wv_hbm, wv_ref), (wk_hbm, wk_ref)], sems
    )
    x = xs_ref[...].astype(F32)
    prepare(x, x[:1], slice(None), xk_ref, xv_ref, flag_ref)
    copies[0].wait()
    rows = normed_rows(feat_ref[...].astype(F32)).astype(BF)
    copies[1].wait()
    wqt = jnp.transpose(wq_ref[...])
    size = wqt.shape[0] // HEADS
    query = lax.dot_general(wqt, rows, NT, preferred_element_type=F32).astype(BF).astype(F32)
    query = query * (LOG2E / size**0.5)
    high = query.astype(BF)
    low = (query - high.astype(F32)).astype(BF)
    none = jnp.zeros((size, rows.shape[0]), BF)
    for h in range(HEADS):
        span = slice(h * size, (h + 1) * size)
        parts = [high[span], none, low[span], none]
        if h % 2:
            parts = [none, high[span], none, low[span]]
        qt_ref[h] = jnp.concatenate(parts, axis=0)
    copies[2].wait()
    wvt_ref[...] = jnp.transpose(wv_ref[...])
    copies[3].wait()
    attend((xk_ref, xv_ref, flag_ref), qt_ref, wk_ref, wvt_ref, acc_ref, top_ref, True)


def each_part(parts, state_in, qt_ref, wk_ref, wvt_ref, state, xs):
    for here, there in zip(state_in, state):
        there[...] = here[...]

    def step(i, carry):
        for n, part in enumerate(parts):

            @pl.when(i == n)
            def _(part=part):
                x = part[...].astype(F32)
                prepare(x, x[:1], slice(None), *xs)

        attend(xs, qt_ref, wk_ref, wvt_ref, *state, False)
        return carry

    lax.fori_loop(0, len(parts), step, 0)


def more_kernel(count, *refs):
    qt_ref, wk_ref, wvt_ref, acc_in, top_in, acc_ref, top_ref, *xs = refs[count:]
    each_part(
        refs[:count], (acc_in, top_in), qt_ref, wk_ref, wvt_ref, (acc_ref, top_ref), xs
    )


def cross_kernel(slots, slot_ref, local_ref, count_ref, *refs):
    pieces = refs[:slots]
    qt_ref, wk_ref, wvt_ref, out_ref, sel_ref, k_ref, v_ref, o_ref, *xs = refs[slots:]
    blocks = count_ref.shape[0]
    per = out_ref.shape[1] // blocks
    span = CROSS * per
    size = out_ref.shape[0] // HEADS
    place = lax.broadcasted_iota(jnp.int32, (span, out_ref.shape[0]), 0)
    for b in range(blocks):
        for c in range(CROSS):
            n = b * CROSS + c
            for s in range(slots):

                @pl.when(slot_ref[n] == s)
                def _(n=n, s=s):
                    start = pl.multiple_of(local_ref[n] * per, per)
                    sel_ref[n * per : (n + 1) * per, :] = pieces[s][pl.ds(start, per), :]

        x = sel_ref[b * span : (b + 1) * span, :].astype(F32)
        x = jnp.where(place < count_ref[b] * per, x, DEAD)
        prepare(x, x[:1], slice(b * span, (b + 1) * span), *xs)
    keys, vals, ones = keys_values(*xs, wk_ref, wvt_ref)
    k_ref[...] = keys
    for b in range(blocks):
        v_ref[b] = vals[:, b * span : (b + 1) * span]
        o_ref[b] = ones[:, b * span : (b + 1) * span]

    for b in range(blocks):
        scores, probs = [], []
        for h in range(HEADS):
            pair = k_ref[b * span : (b + 1) * span, h // 2 * 2 * size : (h // 2 + 1) * 2 * size]
            s = jnp.dot(
                jnp.concatenate([pair, pair], axis=1),
                qt_ref[h, :, b * per : (b + 1) * per],
                preferred_element_type=F32,
            )
            scores.append(s)
        for s in scores:
            probs.append(jnp.exp2(s - jnp.max(s, axis=0, keepdims=True)).astype(BF))
        for h, p in enumerate(probs):
            val = jnp.concatenate([v_ref[b, h * size : (h + 1) * size], o_ref[b]], axis=0)
            added = jnp.dot(val, p, preferred_element_type=F32)
            out_ref[h * size : (h + 1) * size, b * per : (b + 1) * per] = (
                added[:size] / added[size : size + 1]
            )


def last_kernel(count, *refs):
    parts = refs[:count]
    (
        qt_ref, wk_ref, wvt_ref, acc_in, top_in, cross_ref, feat_hbm, wo_hbm, wu_hbm, wd_hbm,
        out_ref, acc_ref, top_ref, feat_ref, wo_ref, wu_ref, wd_ref, sems, *xs,
    ) = refs[count:]
    copies = start_copies(
        [(feat_hbm, feat_ref), (wo_hbm, wo_ref), (wu_hbm, wu_ref), (wd_hbm, wd_ref)], sems
    )
    half = parts[0].shape[0]
    for n, part in enumerate(parts):
        x = part[...].astype(F32)
        prepare(x, x[:1], slice(n * half, (n + 1) * half), *xs)
    acc_ref[...] = acc_in[...]
    top_ref[...] = top_in[...]
    attend(xs, qt_ref, wk_ref, wvt_ref, acc_ref, top_ref, False)
    size = cross_ref.shape[0] // HEADS
    mixed = jnp.concatenate(
        [
            (
                acc_ref[h, :size] / acc_ref[h, size : size + 1]
                + cross_ref[h * size : (h + 1) * size, :]
            ).astype(BF)
            for h in range(HEADS)
        ],
        axis=0,
    )
    copies[0].wait()
    copies[1].wait()
    resid = (
        feat_ref[...].astype(F32)
        + jnp.dot(jnp.transpose(mixed), wo_ref[...], preferred_element_type=F32)
    ).astype(BF)
    wide = resid.astype(F32)
    rows = normed_rows(wide).astype(BF)
    copies[2].wait()
    copies[3].wait()
    step = 512
    total = wide
    for f in range(0, wu_ref.shape[1], step):
        hidden = jax.nn.gelu(
            jnp.dot(rows, wu_ref[:, f : f + step], preferred_element_type=F32)
        ).astype(BF)
        total = total + jnp.dot(hidden, wd_ref[f : f + step, :], preferred_element_type=F32)
    out_ref[...] = total.astype(BF)


def ring_order(mesh):
    count = mesh.shape["dom"]
    plain = list(range(count))
    line = mesh.devices[(0,) * (mesh.devices.ndim - 1)]
    at = [getattr(d, "coords", None) for d in line]
    if any(c is None for c in at):
        return plain
    axes = [i for i in range(3) if len({c[i] for c in at}) > 1]
    if len(axes) != 2:
        return plain
    sizes = [len({c[i] for c in at}) for i in axes]
    if sizes[0] * sizes[1] != count:
        return plain
    if sizes[0] % 2:
        axes, sizes = axes[::-1], sizes[::-1]
    if sizes[0] % 2:
        return plain
    low = [min(c[i] for c in at) for i in axes]
    where = {tuple(c[i] - lo for i, lo in zip(axes, low)): n for n, c in enumerate(at)}
    walk = []
    for row in range(sizes[0]):
        columns = list(range(1 if row else 0, sizes[1]))
        walk += [(row, col) for col in (columns[::-1] if row % 2 else columns)]
    walk += [(row, 0) for row in range(sizes[0] - 1, 0, -1)]
    if any(w not in where for w in walk):
        return plain
    return [where[w] for w in walk]


def make_body(order):
    count = len(order)
    forward = [(order[i], order[(i + 1) % count]) for i in range(count)]
    backward = [(b, a) for a, b in forward]

    def body(
        features, w_query, w_key, w_value, w_out, w_up, w_down, block_len, cross_blocks, cross_count
    ):
        rows, width = features.shape
        blocks = block_len.shape[0]
        groups = lax.axis_size("group")
        sds = jax.ShapeDtypeStruct
        size = width // HEADS
        dma = pltpu.SemaphoreType.DMA

        def rows_scratch(n):
            return [pltpu.VMEM((n, width), BF), pltpu.VMEM((n, width), BF), pltpu.VMEM((n, 128), BF)]

        (mine,) = kernel_call(
            norm_kernel, (block_len, features), [hbm(), hbm()], [sds((rows, width), BF)],
            rows * width * 4,
            [pltpu.SMEM((blocks,), jnp.int32), pltpu.VMEM((rows, width), BF), dma((blocks + 1,))],
        )

        def hop(x, pairs):
            return lax.ppermute(x, "dom", pairs)

        ahead = behind = mine
        arrived = []
        for _ in range(count // 2 - 1):
            ahead = hop(ahead, forward)
            behind = hop(behind, backward)
            arrived.append((ahead, behind))
        half = rows // 2
        arrived.append((hop(ahead[:half], forward), hop(behind[half:], backward)))

        same = [mine] + [
            lax.ppermute(mine, "group", [(i, (i - 2 * k) % groups) for i in range(groups)])
            for k in range(1, groups // 2)
        ]
        swap = [(i, i ^ 1) for i in range(groups)]
        pieces = same + [lax.ppermute(s, "group", swap) for s in same]
        here = lax.axis_index("group")
        per_group = lax.axis_size("dom") * blocks
        chosen = cross_blocks.reshape(-1)
        group = chosen // per_group
        slot = (group // 2 - here // 2) % (groups // 2) + jnp.where(
            group % 2 == here % 2, 0, groups // 2
        )
        local = chosen % blocks

        state = [sds((HEADS, size + ONES, rows), F32), sds((HEADS, rows), F32)]
        work = 2 * 4 * rows * rows * width * 2
        square = sds((width, width), BF)
        qt, wk, wvt, acc, top = kernel_call(
            first_kernel,
            (mine, features, w_query, w_key, w_value),
            [vmem()] + [hbm()] * 4,
            [sds((HEADS, 4 * size, rows), BF), square, square, *state],
            work,
            [
                pltpu.VMEM((rows, width), BF),
                pltpu.VMEM((width, width), BF),
                pltpu.VMEM((width, width), BF),
                dma((4,)),
                *rows_scratch(rows),
            ],
        )
        cross = None
        for parts in arrived[:-1]:
            acc, top = kernel_call(
                lambda *refs, n=len(parts): more_kernel(n, *refs),
                (*parts, qt, wk, wvt, acc, top),
                [vmem()] * (len(parts) + 5),
                state,
                2 * work,
                rows_scratch(rows),
                {len(parts) + 3: 0, len(parts) + 4: 1},
            )
        picked = rows * CROSS
        span = picked // blocks
        (cross,) = kernel_call(
            lambda *refs, n=len(pieces): cross_kernel(n, *refs),
            (slot, local, cross_count, *pieces, qt, wk, wvt),
            [smem()] * 3 + [vmem()] * (len(pieces) + 3),
            [sds((width, rows), F32)],
            work,
            [
                pltpu.VMEM((picked, width), BF),
                pltpu.VMEM((picked, width), BF),
                pltpu.VMEM((blocks, width, span), BF),
                pltpu.VMEM((blocks, ONES, span), BF),
                *rows_scratch(picked),
            ],
        )
        parts = arrived[-1]
        (out,) = kernel_call(
            lambda *refs, n=len(parts): last_kernel(n, *refs),
            (*parts, qt, wk, wvt, acc, top, cross, features, w_out, w_up, w_down),
            [vmem()] * (len(parts) + 6) + [hbm()] * 4,
            [sds((rows, width), BF)],
            2 * work,
            [
                *(pltpu.VMEM(s.shape, F32) for s in state),
                pltpu.VMEM((rows, width), BF),
                *(pltpu.VMEM(w.shape, BF) for w in (w_out, w_up, w_down)),
                dma((4,)),
                *rows_scratch(rows),
            ],
        )
        return out

    return body


def solution(mesh):
    order = ring_order(mesh)
    inner = make_body(order)

    return jax.shard_map(
        inner,
        mesh=mesh,
        in_specs=(
            P(("group", "dom"), None),
            P(),
            P(),
            P(),
            P(),
            P(),
            P(),
            P(("group", "dom")),
            P(("group", "dom"), None),
            P(("group", "dom")),
        ),
        out_specs=P(("group", "dom"), None),
        check_vma=False,
    )
```

profile of v0, /device:TPU:0, one launch (start us, length us, event | category | flops | bytes accessed | tf_op | source)
XLA Modules:
  0.0 80.0 jit_solution(11970619478750068281)
XLA Ops:
  0.0 0.0 copy-start
  0.0 1.0 %copy-done = bf16[512,512]{1,0:T(8,128)(2,1)S(1)} copy-done((bf16[512,512]{1,0:T(8,128)(2,1)S(1)}, bf16[512,512]{1,0:T(8,128)(2,1)}, u32[]{:S(2)}) %copy-start) | copy-done | bytes 524312
  1.0 0.0 copy-start.3
  1.0 0.7 copy-done.3
  1.7 1.2 %shard_map.100.xs_ref.refs_3_ = bf16[512,512]{1,0:T(8,128)(2,1)S(1)} custom-call(s32[4]{0:T(128)S(1)} %copy-done.3, bf16[512,512]{1,0:T(8,128)(2,1)S(1)} %copy-done), custom_call_target="tpu_custom_call" | custom-call | flops 1048576 | bytes 1048592 | tf_op jit(solution)/shard_map/pallas_call | solution.py:36
  2.9 3.0 %collective-permute-start.8 = (bf16[512,512]{1,0:T(8,128)(2,1)S(1)}, bf16[512,512]{1,0:T(8,128)(2,1)S(1)}, u32[]{:S(2)}, u32[]{:S(2)}) collective-permute-start(bf16[512,512]{1,0:T(8,128)(2,1)S(1)} %shard_map.100.xs_ref.refs_3_), channel_id=1, source_target_pairs={{0,16},{8,24},{16,0},{24,8},{1,17},{9,25},{17,1},{25,9},{2,18},{10... | collective-permute-start | bytes 1572872 | tf_op jit(solution)/shard_map/ppermute | solution.py:331
  5.9 1.6 %collective-permute-start = (bf16[512,512]{1,0:T(8,128)(2,1)S(1)}, bf16[512,512]{1,0:T(8,128)(2,1)S(1)}, u32[]{:S(2)}, u32[]{:S(2)}) collective-permute-start(bf16[512,512]{1,0:T(8,128)(2,1)S(1)} %shard_map.100.xs_ref.refs_3_), channel_id=1, source_target_pairs={{0,2},{2,4},{4,6},{6,7},{7,5},{5,3},{3,1},{1,0},{8,10},{10,12},{12... | collective-permute-start | bytes 1572872 | tf_op jit(solution)/shard_map/ppermute | solution.py:319
  7.5 0.4 collective-permute-start.4
  7.9 0.0 collective-permute-start.9
  8.0 0.8 copy.18
  8.7 0.1 reshape.3
  8.8 9.0 %collective-permute-done.8.refs_4_ = bf16[512,512]{1,0:T(8,128)(2,1)S(1)} collective-permute-done((bf16[512,512]{1,0:T(8,128)(2,1)S(1)}, bf16[512,512]{1,0:T(8,128)(2,1)S(1)}, u32[]{:S(2)}, u32[]{:S(2)}) %collective-permute-start.8) | collective-permute-done | bytes 524320 | tf_op jit(solution)/shard_map/ppermute | solution.py:331
  17.8 0.0 collective-permute-start.10
  17.8 1.5 %collective-permute-done.refs_0_ = bf16[512,512]{1,0:T(8,128)(2,1)S(1)} collective-permute-done((bf16[512,512]{1,0:T(8,128)(2,1)S(1)}, bf16[512,512]{1,0:T(8,128)(2,1)S(1)}, u32[]{:S(2)}, u32[]{:S(2)}) %collective-permute-start) | collective-permute-done | bytes 524320 | tf_op jit(solution)/shard_map/ppermute | solution.py:319
  19.3 1.6 %collective-permute-start.1 = (bf16[512,512]{1,0:T(8,128)(2,1)S(1)}, bf16[512,512]{1,0:T(8,128)(2,1)S(1)}, u32[]{:S(2)}, u32[]{:S(2)}) collective-permute-start(bf16[512,512]{1,0:T(8,128)(2,1)S(1)} %collective-permute-done.refs_0_), channel_id=1, source_target_pairs={{0,2},{2,4},{4,6},{6,7},{7,5},{5,3},{3,1},{1,0},{8,10},{10,12},{12... | collective-permute-start | bytes 1572872 | tf_op jit(solution)/shard_map/ppermute | solution.py:319
  20.9 0.0 collective-permute-done.4.refs_1_
  20.9 0.5 collective-permute-start.5
  21.3 1.0 %copy-done.1 = bf16[512,512]{1,0:T(8,128)(2,1)S(1)} copy-done((bf16[512,512]{1,0:T(8,128)(2,1)S(1)}, bf16[512,512]{1,0:T(8,128)(2,1)}, u32[]{:S(2)}) %copy-start.1) | copy-done | bytes 524312
  22.4 0.0 copy-start.6
  22.4 1.0 %copy-done.6 = bf16[512,512]{1,0:T(8,128)(2,1)S(1)} copy-done((bf16[512,512]{1,0:T(8,128)(2,1)S(1)}, bf16[512,512]{1,0:T(8,128)(2,1)}, u32[]{:S(2)}) %copy-start.6) | copy-done | bytes 524312
  23.4 0.0 copy-start.7
  23.4 1.0 %copy-done.7 = bf16[512,512]{1,0:T(8,128)(2,1)S(1)} copy-done((bf16[512,512]{1,0:T(8,128)(2,1)S(1)}, bf16[512,512]{1,0:T(8,128)(2,1)}, u32[]{:S(2)}) %copy-start.7) | copy-done | bytes 524312
  24.5 0.0 copy-start.8
  24.5 1.0 %copy-done.8 = bf16[512,512]{1,0:T(8,128)(2,1)S(1)} copy-done((bf16[512,512]{1,0:T(8,128)(2,1)S(1)}, bf16[512,512]{1,0:T(8,128)(2,1)}, u32[]{:S(2)}) %copy-start.8) | copy-done | bytes 524312
  25.5 6.0 %shard_map.101 = (bf16[8,256,512]{2,1,0:T(8,128)(2,1)S(1)}, bf16[512,512]{1,0:T(8,128)(2,1)S(1)}, bf16[512,512]{1,0:T(8,128)(2,1)S(1)}, f32[8,80,512]{2,1,0:T(8,128)S(1)}, f32[8,512]{1,0:T(8,128)S(1)}) custom-call(bf16[512,512]{1,0:T(8,128)(2,1)S(1)} %shard_map.100.xs_ref.refs_3_, bf16[512,512]{1,0:T(8,128)(2,1)S(1)} %copy-done.1, ...), custom_call_target="tpu_custom_call" | custom-call | flops 2147483648 | bytes 7094272 | tf_op jit(solution)/shard_map/pallas_call | solution.py:36
  31.5 0.0 copy-start.10
  31.5 9.9 %shard_map.102 = (f32[8,80,512]{2,1,0:T(8,128)S(1)}, f32[8,512]{1,0:T(8,128)S(1)}) custom-call(bf16[512,512]{1,0:T(8,128)(2,1)S(1)} %collective-permute-done.refs_0_, bf16[512,512]{1,0:T(8,128)(2,1)S(1)} %collective-permute-done.4.refs_1_, bf16[8,256,512]{2,1,0:T(8,128)(2,1)S(1)} %get-tuple-element.16.refs_2_.refs_7_, ...), custom_call_target="tpu_custom_call", output_to_operand_aliasing={{0}: (5, {}), {1}: (6, {})} | custom-call | flops 4294967296 | bytes 6848512 | tf_op jit(solution)/shard_map/pallas_call | solution.py:36
  41.4 0.0 collective-permute-done.1.refs_0_
  41.4 1.6 %collective-permute-start.2 = (bf16[512,512]{1,0:T(8,128)(2,1)S(1)}, bf16[512,512]{1,0:T(8,128)(2,1)S(1)}, u32[]{:S(2)}, u32[]{:S(2)}) collective-permute-start(bf16[512,512]{1,0:T(8,128)(2,1)S(1)} %collective-permute-done.1.refs_0_), channel_id=1, source_target_pairs={{0,2},{2,4},{4,6},{6,7},{7,5},{5,3},{3,1},{1,0},{8,10},{10,12},{12... | collective-permute-start | bytes 1572872 | tf_op jit(solution)/shard_map/ppermute | solution.py:319
  43.0 0.0 collective-permute-done.5.refs_1_
  43.0 0.4 collective-permute-start.6
  43.5 0.0 collective-permute-done.9.refs_5_
  43.5 0.0 collective-permute-done.10.refs_6_
  43.5 0.0 copy-done.10
  43.5 4.8 %shard_map.105.refs_7_ = f32[512,512]{1,0:T(8,128)S(1)} custom-call(s32[8]{0:T(128)S(1)} %get-tuple-element.28.refs_0_, s32[8]{0:T(128)S(1)} %get-tuple-element.27.refs_1_, s32[4]{0:T(128)S(1)} %copy-done.10, bf16[512,512]{1,0:T(8,128)(2,1)S(1)} %shard_map.100.xs_ref.refs_3_, bf16[512,512]{1,0:T(8,128)(2,1)S(1)} %collective-permute-done.8.refs_4_, ...), custom_call_target="tpu_custom_call" | custom-call | flops 2147483648 | bytes 6291536 | tf_op jit(solution)/shard_map/pallas_call | solution.py:36
  48.3 9.9 %shard_map.103 = (f32[8,80,512]{2,1,0:T(8,128)S(1)}, f32[8,512]{1,0:T(8,128)S(1)}) custom-call(bf16[512,512]{1,0:T(8,128)(2,1)S(1)} %collective-permute-done.1.refs_0_, bf16[512,512]{1,0:T(8,128)(2,1)S(1)} %collective-permute-done.5.refs_1_, ...), custom_call_target="tpu_custom_call", output_to_operand_aliasing={{0}: (5, {}), {1}: (6, {})} | custom-call | flops 4294967296 | bytes 6848512 | tf_op jit(solution)/shard_map/pallas_call | solution.py:36
  58.2 0.0 collective-permute-done.2.refs_0_
  58.2 1.6 %collective-permute-start.3 = (bf16[256,512]{1,0:T(8,128)(2,1)S(1)}, bf16[256,512]{1,0:T(8,128)(2,1)S(1)}, u32[]{:S(2)}, u32[]{:S(2)}) collective-permute-start(bf16[256,512]{1,0:T(8,128)(2,1)S(1)} %slice.8), channel_id=1, source_target_pairs={{0,2},{2,4},{4,6},{6,7},{7,5},{5,3},{3,1},{1,0},{8,10},{10,12},{12... | collective-permute-start | bytes 786440 | tf_op jit(solution)/shard_map/ppermute | solution.py:319
  59.8 0.0 collective-permute-done.6.refs_1_
  59.8 0.7 collective-permute-start.7
  60.6 9.9 %shard_map.104 = (f32[8,80,512]{2,1,0:T(8,128)S(1)}, f32[8,512]{1,0:T(8,128)S(1)}) custom-call(bf16[512,512]{1,0:T(8,128)(2,1)S(1)} %collective-permute-done.2.refs_0_, bf16[512,512]{1,0:T(8,128)(2,1)S(1)} %collective-permute-done.6.refs_1_, ...), custom_call_target="tpu_custom_call", output_to_operand_aliasing={{0}: (5, {}), {1}: (6, {})} | custom-call | flops 4294967296 | bytes 6848512 | tf_op jit(solution)/shard_map/pallas_call | solution.py:36
  70.5 0.0 collective-permute-done.3.refs_0_
  70.5 0.0 collective-permute-done.7.refs_1_
  70.5 0.0 copy-done.2
  70.5 0.0 copy-done.4
  70.5 0.0 copy-done.5
  70.5 0.0 copy-done.9
  70.5 9.3 %shard_map.106 = bf16[512,512]{1,0:T(8,128)(2,1)} custom-call(bf16[256,512]{1,0:T(8,128)(2,1)S(1)} %collective-permute-done.3.refs_0_, bf16[256,512]{1,0:T(8,128)(2,1)S(1)} %collective-permute-done.7.refs_1_, bf16[8,256,512]{2,1,0:T(8,128)(2,1)S(1)} %get-tuple-element.16.refs_2_.refs_7_, bf16[512,512]{1,0:T(8,128)(2,1)S(1)} %get-tuple-element.17.refs_3_.refs_8_, ...), custom_call_target="tpu_custom_call" | custom-call | flops 4294967296 | bytes 11812864 | tf_op jit(solution)/shard_map/pallas_call | solution.py:36
  (8 shorter events, 0.1 us)
Async XLA Ops:
  0.0 1.0 %copy-start = (bf16[512,512]{1,0:T(8,128)(2,1)S(1)}, bf16[512,512]{1,0:T(8,128)(2,1)}, u32[]{:S(2)}) copy-start(bf16[512,512]{1,0:T(8,128)(2,1)} %refs_8_.1) | copy-start | bytes 1572868
  1.0 0.7 copy-start.3
  2.9 15.0 %collective-permute-start.8 = (bf16[512,512]{1,0:T(8,128)(2,1)S(1)}, bf16[512,512]{1,0:T(8,128)(2,1)S(1)}, u32[]{:S(2)}, u32[]{:S(2)}) collective-permute-start(bf16[512,512]{1,0:T(8,128)(2,1)S(1)} %shard_map.100.xs_ref.refs_3_), channel_id=1, source_target_pairs={{0,16},{8,24},{16,0},{24,8},{1,17},{9,25},{17,1},{25,9},{2,18},{10... | collective-permute-start | bytes 1572872 | tf_op jit(solution)/shard_map/ppermute | solution.py:331
  5.9 13.4 %collective-permute-start = (bf16[512,512]{1,0:T(8,128)(2,1)S(1)}, bf16[512,512]{1,0:T(8,128)(2,1)S(1)}, u32[]{:S(2)}, u32[]{:S(2)}) collective-permute-start(bf16[512,512]{1,0:T(8,128)(2,1)S(1)} %shard_map.100.xs_ref.refs_3_), channel_id=1, source_target_pairs={{0,2},{2,4},{4,6},{6,7},{7,5},{5,3},{3,1},{1,0},{8,10},{10,12},{12... | collective-permute-start | bytes 1572872 | tf_op jit(solution)/shard_map/ppermute | solution.py:319
  7.5 13.4 %collective-permute-start.4 = (bf16[512,512]{1,0:T(8,128)(2,1)S(1)}, bf16[512,512]{1,0:T(8,128)(2,1)S(1)}, u32[]{:S(2)}, u32[]{:S(2)}) collective-permute-start(bf16[512,512]{1,0:T(8,128)(2,1)S(1)} %shard_map.100.xs_ref.refs_3_), channel_id=1, source_target_pairs={{2,0},{4,2},{6,4},{7,6},{5,7},{3,5},{1,3},{0,1},{10,8},{12,10},{14... | collective-permute-start | bytes 1572872 | tf_op jit(solution)/shard_map/ppermute | solution.py:319
  7.9 35.5 %collective-permute-start.9 = (bf16[512,512]{1,0:T(8,128)(2,1)S(1)}, bf16[512,512]{1,0:T(8,128)(2,1)S(1)}, u32[]{:S(2)}, u32[]{:S(2)}) collective-permute-start(bf16[512,512]{1,0:T(8,128)(2,1)S(1)} %shard_map.100.xs_ref.refs_3_), channel_id=1, source_target_pairs={{0,8},{8,0},{16,24},{24,16},{1,9},{9,1},{17,25},{25,17},{2,10},{10... | collective-permute-start | bytes 1572872 | tf_op jit(solution)/shard_map/ppermute | solution.py:335
  17.8 25.6 %collective-permute-start.10 = (bf16[512,512]{1,0:T(8,128)(2,1)S(1)}, bf16[512,512]{1,0:T(8,128)(2,1)S(1)}, u32[]{:S(2)}, u32[]{:S(2)}) collective-permute-start(bf16[512,512]{1,0:T(8,128)(2,1)S(1)} %collective-permute-done.8.refs_4_), channel_id=1, source_target_pairs={{0,8},{8,0},{16,24},{24,16},{1,9},{9,1},{17,25},{25,17},{2,10},{10... | collective-permute-start | bytes 1572872 | tf_op jit(solution)/shard_map/ppermute | solution.py:335
  19.3 22.1 %collective-permute-start.1 = (bf16[512,512]{1,0:T(8,128)(2,1)S(1)}, bf16[512,512]{1,0:T(8,128)(2,1)S(1)}, u32[]{:S(2)}, u32[]{:S(2)}) collective-permute-start(bf16[512,512]{1,0:T(8,128)(2,1)S(1)} %collective-permute-done.refs_0_), channel_id=1, source_target_pairs={{0,2},{2,4},{4,6},{6,7},{7,5},{5,3},{3,1},{1,0},{8,10},{10,12},{12... | collective-permute-start | bytes 1572872 | tf_op jit(solution)/shard_map/ppermute | solution.py:319
  20.9 22.1 %collective-permute-start.5 = (bf16[512,512]{1,0:T(8,128)(2,1)S(1)}, bf16[512,512]{1,0:T(8,128)(2,1)S(1)}, u32[]{:S(2)}, u32[]{:S(2)}) collective-permute-start(bf16[512,512]{1,0:T(8,128)(2,1)S(1)} %collective-permute-done.4.refs_1_), channel_id=1, source_target_pairs={{2,0},{4,2},{6,4},{7,6},{5,7},{3,5},{1,3},{0,1},{10,8},{12,10},{14... | collective-permute-start | bytes 1572872 | tf_op jit(solution)/shard_map/ppermute | solution.py:319
  21.3 1.0 %copy-start.1 = (bf16[512,512]{1,0:T(8,128)(2,1)S(1)}, bf16[512,512]{1,0:T(8,128)(2,1)}, u32[]{:S(2)}) copy-start(bf16[512,512]{1,0:T(8,128)(2,1)} %refs_8_.1) | copy-start | bytes 1572868
  22.4 1.0 %copy-start.6 = (bf16[512,512]{1,0:T(8,128)(2,1)S(1)}, bf16[512,512]{1,0:T(8,128)(2,1)}, u32[]{:S(2)}) copy-start(bf16[512,512]{1,0:T(8,128)(2,1)} %wq_hbm.1) | copy-start | bytes 1572868
  23.4 1.0 %copy-start.7 = (bf16[512,512]{1,0:T(8,128)(2,1)S(1)}, bf16[512,512]{1,0:T(8,128)(2,1)}, u32[]{:S(2)}) copy-start(bf16[512,512]{1,0:T(8,128)(2,1)} %wk_hbm.1) | copy-start | bytes 1572868
  24.5 1.0 %copy-start.8 = (bf16[512,512]{1,0:T(8,128)(2,1)S(1)}, bf16[512,512]{1,0:T(8,128)(2,1)}, u32[]{:S(2)}) copy-start(bf16[512,512]{1,0:T(8,128)(2,1)} %wv_hbm.1) | copy-start | bytes 1572868
  31.5 12.0 %copy-start.10 = (s32[4]{0:T(128)S(1)}, s32[4]{0:T(128)}, u32[]{:S(2)}) copy-start(s32[4]{0:T(128)} %refs_2_.1) | copy-start | bytes 52
  41.4 16.8 %collective-permute-start.2 = (bf16[512,512]{1,0:T(8,128)(2,1)S(1)}, bf16[512,512]{1,0:T(8,128)(2,1)S(1)}, u32[]{:S(2)}, u32[]{:S(2)}) collective-permute-start(bf16[512,512]{1,0:T(8,128)(2,1)S(1)} %collective-permute-done.1.refs_0_), channel_id=1, source_target_pairs={{0,2},{2,4},{4,6},{6,7},{7,5},{5,3},{3,1},{1,0},{8,10},{10,12},{12... | collective-permute-start | bytes 1572872 | tf_op jit(solution)/shard_map/ppermute | solution.py:319
  43.0 16.8 %collective-permute-start.6 = (bf16[512,512]{1,0:T(8,128)(2,1)S(1)}, bf16[512,512]{1,0:T(8,128)(2,1)S(1)}, u32[]{:S(2)}, u32[]{:S(2)}) collective-permute-start(bf16[512,512]{1,0:T(8,128)(2,1)S(1)} %collective-permute-done.5.refs_1_), channel_id=1, source_target_pairs={{2,0},{4,2},{6,4},{7,6},{5,7},{3,5},{1,3},{0,1},{10,8},{12,10},{14... | collective-permute-start | bytes 1572872 | tf_op jit(solution)/shard_map/ppermute | solution.py:319
  58.2 12.3 %collective-permute-start.3 = (bf16[256,512]{1,0:T(8,128)(2,1)S(1)}, bf16[256,512]{1,0:T(8,128)(2,1)S(1)}, u32[]{:S(2)}, u32[]{:S(2)}) collective-permute-start(bf16[256,512]{1,0:T(8,128)(2,1)S(1)} %slice.8), channel_id=1, source_target_pairs={{0,2},{2,4},{4,6},{6,7},{7,5},{5,3},{3,1},{1,0},{8,10},{10,12},{12... | collective-permute-start | bytes 786440 | tf_op jit(solution)/shard_map/ppermute | solution.py:319
  59.8 10.6 %collective-permute-start.7 = (bf16[256,512]{1,0:T(8,128)(2,1)S(1)}, bf16[256,512]{1,0:T(8,128)(2,1)S(1)}, u32[]{:S(2)}, u32[]{:S(2)}) collective-permute-start(bf16[256,512]{1,0:T(8,128)(2,1)S(1)} %slice.9), channel_id=1, source_target_pairs={{2,0},{4,2},{6,4},{7,6},{5,7},{3,5},{1,3},{0,1},{10,8},{12,10},{14... | collective-permute-start | bytes 786440 | tf_op jit(solution)/shard_map/ppermute | solution.py:319
  60.6 9.9 %copy-start.2 = (bf16[512,512]{1,0:T(8,128)(2,1)S(1)}, bf16[512,512]{1,0:T(8,128)(2,1)}, u32[]{:S(2)}) copy-start(bf16[512,512]{1,0:T(8,128)(2,1)} %refs_8_.1) | copy-start | bytes 1572868
  60.6 9.9 %copy-start.4 = (bf16[512,2048]{1,0:T(8,128)(2,1)S(1)}, bf16[512,2048]{1,0:T(8,128)(2,1)}, u32[]{:S(2)}) copy-start(bf16[512,2048]{1,0:T(8,128)(2,1)} %refs_10_.1) | copy-start | bytes 6291460
  60.6 9.9 %copy-start.5 = (bf16[2048,512]{1,0:T(8,128)(2,1)S(1)}, bf16[2048,512]{1,0:T(8,128)(2,1)}, u32[]{:S(2)}) copy-start(bf16[2048,512]{1,0:T(8,128)(2,1)} %refs_11_.1) | copy-start | bytes 6291460
  60.6 9.9 %copy-start.9 = (bf16[512,512]{1,0:T(8,128)(2,1)S(1)}, bf16[512,512]{1,0:T(8,128)(2,1)}, u32[]{:S(2)}) copy-start(bf16[512,512]{1,0:T(8,128)(2,1)} %refs_9_.1) | copy-start | bytes 1572868
where the time goes:
time: 80.4 us; the launch traced here: 80 us
  Pallas kernels  50.8 us (63%)
  starting transfers between devices  11.5 us (14%)
  waiting for transfers between devices  10.5 us (13%)
  local copies, waits for them, and re-layouts  6.77 us (8%)
    pallas_call x7, Pallas kernels, kernel_call(): pl.pallas_call(kernel, out_shape=tuple(outs), in_specs=specs, out_specs=t...  50.8 us
    ppermute x1, waiting for transfers between devices, body(): lax.ppermute(mine, 'group', [(i, (i - 2 * k) % groups) for i in range(gro...  9.01 us
    ppermute x8, starting transfers between devices, hop(): return lax.ppermute(x, 'dom', pairs)  8.48 us
    unnamed x23, local copies, waits for them, and re-layouts  6.65 us
    ppermute x1, starting transfers between devices, body(): lax.ppermute(mine, 'group', [(i, (i - 2 * k) % groups) for i in range(gro...  3.03 us
  transfers between devices with their start and end apart: 11, of which 2 were waited for; matrix products, arithmetic and copies ran while one was open for 1% of the time, Pallas kernels for 50%

commit v1 on v0

--- a/solution.py
+++ b/solution.py
@@ -72,55 +72,74 @@
         out_ref[span, :] = jnp.where(place < len_ref[b], row, DEAD).astype(BF)
 
 
-def prepare(x, spare, span, xk_ref, xv_ref, flag_ref):
-    live = x[:, :1] < DEAD_FROM
-    xk_ref[span, :] = jnp.where(live, x, spare).astype(BF)
-    xv_ref[span, :] = jnp.where(live, x, 0.0).astype(BF)
-    flag_ref[span, :] = jnp.broadcast_to(
-        jnp.where(live, 1.0, 0.0), (x.shape[0], flag_ref.shape[1])
-    ).astype(BF)
-
-
-def keys_values(xk_ref, xv_ref, flag_ref, wk_ref, wvt_ref):
-    keys = jnp.dot(xk_ref[...], wk_ref[...], preferred_element_type=F32).astype(BF)
-    vals = lax.dot_general(wvt_ref[...], xv_ref[...], NT, preferred_element_type=F32).astype(BF)
-    lane = lax.broadcasted_iota(jnp.int32, (ONES, flag_ref.shape[1]), 1)
+def load_part(x, spare, span, wk_ref, wvt_ref, k_ref, v_ref):
+    live = x[:, :1] < jnp.asarray(DEAD_FROM, BF)
+    rows = jnp.where(live, x, spare)
+    flag = jnp.broadcast_to(jnp.where(live, jnp.ones((), BF), jnp.zeros((), BF)), (x.shape[0], 128))
+    lane = lax.broadcasted_iota(jnp.int32, (ONES, 128), 1)
     ones = lax.dot_general(
-        jnp.where(lane == 0, 1.0, 0.0).astype(BF), flag_ref[...], NT, preferred_element_type=F32
-    ).astype(BF)
-    return keys, vals, ones
-
-
-def attend(xs, qt_ref, wk_ref, wvt_ref, acc_ref, top_ref, first):
-    keys, vals, ones = keys_values(*xs, wk_ref, wvt_ref)
+        jnp.where(lane == 0, 1.0, 0.0).astype(BF), flag, NT, preferred_element_type=F32
+    )
+    keys = jnp.dot(rows, wk_ref[...], preferred_element_type=F32).astype(BF)
+    vals = lax.dot_general(wvt_ref[...], rows, NT, preferred_element_type=F32)
+    vals = (vals * ones[:1]).astype(BF)
+    ones = ones.astype(BF)
     size = vals.shape[0] // HEADS
+    for pair in range(HEADS // 2):
+        k_ref[pair, span, :] = keys[:, pair * 2 * size : (pair + 1) * 2 * size]
     for h in range(HEADS):
-        pair = keys[:, h // 2 * 2 * size : (h // 2 + 1) * 2 * size]
-        s = jnp.dot(
-            jnp.concatenate([pair, pair], axis=1), qt_ref[h], preferred_element_type=F32
-        )
-        top = jnp.max(s, axis=0, keepdims=True)
-        if not first:
-            before = top_ref[h : h + 1, :]
+        v_ref[h, :size, span] = vals[h * size : (h + 1) * size]
+        v_ref[h, size:, span] = ones
+
+
+def attend(qt_ref, k_ref, v_ref, even_ref, odd_ref, old, new):
+    count = k_ref.shape[1]
+    step = min(512, count)
+
+    def scores(h, j, out_ref, top):
+        pair = k_ref[h // 2 if isinstance(h, int) else lax.div(h, 2), j : j + step, :]
+        s = jnp.dot(jnp.concatenate([pair, pair], axis=1), qt_ref[h], preferred_element_type=F32)
+        out_ref[j : j + step, :] = s
+        found = jnp.max(s, axis=0, keepdims=True)
+        return found if top is None else jnp.maximum(top, found)
+
+    def stage(h, in_ref, top, following, out_ref):
+        total = None
+        if old is not None:
+            before = old[1][pl.ds(h, 1), :]
             top = jnp.maximum(before, top)
-        p = jnp.exp2(s - top).astype(BF)
-        val = jnp.concatenate([vals[h * size : (h + 1) * size], ones], axis=0)
-        added = jnp.dot(val, p, preferred_element_type=F32)
-        if not first:
-            added = acc_ref[h] * jnp.exp2(before - top) + added
-        acc_ref[h] = added
-        top_ref[h : h + 1, :] = top
+            total = old[0][h] * jnp.exp2(before - top)
+        new[1][pl.ds(h, 1), :] = top
+        found = None
+        for j in range(0, count, step):
+            if following is not None:
+                found = scores(following, j, out_ref, found)
+            p = jnp.exp2(in_ref[j : j + step, :] - top).astype(BF)
+            added = jnp.dot(v_ref[h, :, j : j + step], p, preferred_element_type=F32)
+            total = added if total is None else total + added
+        new[0][h] = total
+        return found
+
+    def two(i, top):
+        h = 2 * i
+        top = stage(h, even_ref, top, h + 1, odd_ref)
+        return stage(h + 1, odd_ref, top, h + 2, even_ref)
+
+    top = None
+    for j in range(0, count, step):
+        top = scores(0, j, even_ref, top)
+    top = lax.fori_loop(0, HEADS // 2 - 1, two, top)
+    top = stage(HEADS - 2, even_ref, top, HEADS - 1, odd_ref)
+    stage(HEADS - 1, odd_ref, top, None, None)
 
 
 def first_kernel(
     xs_ref, feat_hbm, wq_hbm, wk_hbm, wv_hbm, qt_ref, wk_ref, wvt_ref, acc_ref, top_ref,
-    feat_ref, wq_ref, wv_ref, sems, xk_ref, xv_ref, flag_ref,
+    feat_ref, wq_ref, wv_ref, sems, *work,
 ):
     copies = start_copies(
         [(feat_hbm, feat_ref), (wq_hbm, wq_ref), (wv_hbm, wv_ref), (wk_hbm, wk_ref)], sems
     )
-    x = xs_ref[...].astype(F32)
-    prepare(x, x[:1], slice(None), xk_ref, xv_ref, flag_ref)
     copies[0].wait()
     rows = normed_rows(feat_ref[...].astype(F32)).astype(BF)
     copies[1].wait()
@@ -140,42 +159,33 @@
     copies[2].wait()
     wvt_ref[...] = jnp.transpose(wv_ref[...])
     copies[3].wait()
-    attend((xk_ref, xv_ref, flag_ref), qt_ref, wk_ref, wvt_ref, acc_ref, top_ref, True)
-
-
-def each_part(parts, state_in, qt_ref, wk_ref, wvt_ref, state, xs):
-    for here, there in zip(state_in, state):
-        there[...] = here[...]
-
-    def step(i, carry):
-        for n, part in enumerate(parts):
-
-            @pl.when(i == n)
-            def _(part=part):
-                x = part[...].astype(F32)
-                prepare(x, x[:1], slice(None), *xs)
-
-        attend(xs, qt_ref, wk_ref, wvt_ref, *state, False)
-        return carry
-
-    lax.fori_loop(0, len(parts), step, 0)
+    x = xs_ref[...]
+    load_part(x, x[:1], slice(None), wk_ref, wvt_ref, *work[:2])
+    attend(qt_ref, *work, None, (acc_ref, top_ref))
+
+
+def all_parts(parts, wk_ref, wvt_ref, k_ref, v_ref):
+    start = 0
+    for part in parts:
+        x = part[...]
+        load_part(x, x[:1], slice(start, start + x.shape[0]), wk_ref, wvt_ref, k_ref, v_ref)
+        start += x.shape[0]
 
 
 def more_kernel(count, *refs):
-    qt_ref, wk_ref, wvt_ref, acc_in, top_in, acc_ref, top_ref, *xs = refs[count:]
-    each_part(
-        refs[:count], (acc_in, top_in), qt_ref, wk_ref, wvt_ref, (acc_ref, top_ref), xs
-    )
+    qt_ref, wk_ref, wvt_ref, acc_in, top_in, acc_ref, top_ref, *work = refs[count:]
+    all_parts(refs[:count], wk_ref, wvt_ref, *work[:2])
+    attend(qt_ref, *work, (acc_in, top_in), (acc_ref, top_ref))
 
 
 def cross_kernel(slots, slot_ref, local_ref, count_ref, *refs):
     pieces = refs[:slots]
-    qt_ref, wk_ref, wvt_ref, out_ref, sel_ref, k_ref, v_ref, o_ref, *xs = refs[slots:]
+    qt_ref, wk_ref, wvt_ref, out_ref, sel_ref, k_ref, v_ref = refs[slots:]
     blocks = count_ref.shape[0]
     per = out_ref.shape[1] // blocks
     span = CROSS * per
     size = out_ref.shape[0] // HEADS
-    place = lax.broadcasted_iota(jnp.int32, (span, out_ref.shape[0]), 0)
+    place = lax.broadcasted_iota(jnp.int32, (span, 1), 0)
     for b in range(blocks):
         for c in range(CROSS):
             n = b * CROSS + c
@@ -186,51 +196,46 @@
                     start = pl.multiple_of(local_ref[n] * per, per)
                     sel_ref[n * per : (n + 1) * per, :] = pieces[s][pl.ds(start, per), :]
 
-        x = sel_ref[b * span : (b + 1) * span, :].astype(F32)
-        x = jnp.where(place < count_ref[b] * per, x, DEAD)
-        prepare(x, x[:1], slice(b * span, (b + 1) * span), *xs)
-    keys, vals, ones = keys_values(*xs, wk_ref, wvt_ref)
-    k_ref[...] = keys
-    for b in range(blocks):
-        v_ref[b] = vals[:, b * span : (b + 1) * span]
-        o_ref[b] = ones[:, b * span : (b + 1) * span]
-
-    for b in range(blocks):
-        scores, probs = [], []
-        for h in range(HEADS):
-            pair = k_ref[b * span : (b + 1) * span, h // 2 * 2 * size : (h // 2 + 1) * 2 * size]
-            s = jnp.dot(
-                jnp.concatenate([pair, pair], axis=1),
-                qt_ref[h, :, b * per : (b + 1) * per],
-                preferred_element_type=F32,
+        used = jnp.where(place < count_ref[b] * per, 0.0, DEAD).astype(BF)
+        x = sel_ref[b * span : (b + 1) * span, :]
+        load_part(
+            jnp.where(used > 0, used, x),
+            x[:1], slice(b * span, (b + 1) * span), wk_ref, wvt_ref, k_ref, v_ref,
+        )
+
+    def scores(h, b):
+        pair = k_ref[h // 2, b * span : (b + 1) * span, :]
+        return jnp.dot(
+            jnp.concatenate([pair, pair], axis=1),
+            qt_ref[h, :, b * per : (b + 1) * per],
+            preferred_element_type=F32,
+        )
+
+    turns = [(h, b) for h in range(HEADS) for b in range(blocks)]
+    lag = 4
+    held = []
+    for n in range(len(turns) + lag):
+        if n < len(turns):
+            held.append(scores(*turns[n]))
+        if n >= lag:
+            h, b = turns[n - lag]
+            s = held[n - lag]
+            p = jnp.exp2(s - jnp.max(s, axis=0, keepdims=True)).astype(BF)
+            added = jnp.dot(
+                v_ref[h, :, b * span : (b + 1) * span], p, preferred_element_type=F32
             )
-            scores.append(s)
-        for s in scores:
-            probs.append(jnp.exp2(s - jnp.max(s, axis=0, keepdims=True)).astype(BF))
-        for h, p in enumerate(probs):
-            val = jnp.concatenate([v_ref[b, h * size : (h + 1) * size], o_ref[b]], axis=0)
-            added = jnp.dot(val, p, preferred_element_type=F32)
             out_ref[h * size : (h + 1) * size, b * per : (b + 1) * per] = (
                 added[:size] / added[size : size + 1]
             )
 
 
 def last_kernel(count, *refs):
-    parts = refs[:count]
     (
-        qt_ref, wk_ref, wvt_ref, acc_in, top_in, cross_ref, feat_hbm, wo_hbm, wu_hbm, wd_hbm,
-        out_ref, acc_ref, top_ref, feat_ref, wo_ref, wu_ref, wd_ref, sems, *xs,
+        qt_ref, wk_ref, wvt_ref, acc_in, top_in, cross_ref, feat_ref, wo_ref, wu_ref, wd_ref,
+        out_ref, acc_ref, top_ref, *work,
     ) = refs[count:]
-    copies = start_copies(
-        [(feat_hbm, feat_ref), (wo_hbm, wo_ref), (wu_hbm, wu_ref), (wd_hbm, wd_ref)], sems
-    )
-    half = parts[0].shape[0]
-    for n, part in enumerate(parts):
-        x = part[...].astype(F32)
-        prepare(x, x[:1], slice(n * half, (n + 1) * half), *xs)
-    acc_ref[...] = acc_in[...]
-    top_ref[...] = top_in[...]
-    attend(xs, qt_ref, wk_ref, wvt_ref, acc_ref, top_ref, False)
+    all_parts(refs[:count], wk_ref, wvt_ref, *work[:2])
+    attend(qt_ref, *work, (acc_in, top_in), (acc_ref, top_ref))
     size = cross_ref.shape[0] // HEADS
     mixed = jnp.concatenate(
         [
@@ -242,16 +247,12 @@
         ],
         axis=0,
     )
-    copies[0].wait()
-    copies[1].wait()
     resid = (
         feat_ref[...].astype(F32)
         + jnp.dot(jnp.transpose(mixed), wo_ref[...], preferred_element_type=F32)
     ).astype(BF)
     wide = resid.astype(F32)
     rows = normed_rows(wide).astype(BF)
-    copies[2].wait()
-    copies[3].wait()
     step = 512
     total = wide
     for f in range(0, wu_ref.shape[1], step):
@@ -306,8 +307,14 @@
         size = width // HEADS
         dma = pltpu.SemaphoreType.DMA
 
-        def rows_scratch(n):
-            return [pltpu.VMEM((n, width), BF), pltpu.VMEM((n, width), BF), pltpu.VMEM((n, 128), BF)]
+        def key_scratch(n):
+            return [
+                pltpu.VMEM((HEADS // 2, n, 2 * size), BF),
+                pltpu.VMEM((HEADS, size + ONES, n), BF),
+            ]
+
+        def work_scratch(n):
+            return key_scratch(n) + [pltpu.VMEM((n, rows), F32)] * 2
 
         (mine,) = kernel_call(
             norm_kernel, (block_len, features), [hbm(), hbm()], [sds((rows, width), BF)],
@@ -356,10 +363,9 @@
                 pltpu.VMEM((width, width), BF),
                 pltpu.VMEM((width, width), BF),
                 dma((4,)),
-                *rows_scratch(rows),
+                *work_scratch(rows),
             ],
         )
-        cross = None
         for parts in arrived[:-1]:
             acc, top = kernel_call(
                 lambda *refs, n=len(parts): more_kernel(n, *refs),
@@ -367,11 +373,10 @@
                 [vmem()] * (len(parts) + 5),
                 state,
                 2 * work,
-                rows_scratch(rows),
+                work_scratch(len(parts) * rows),
                 {len(parts) + 3: 0, len(parts) + 4: 1},
             )
         picked = rows * CROSS
-        span = picked // blocks
         (cross,) = kernel_call(
             lambda *refs, n=len(pieces): cross_kernel(n, *refs),
             (slot, local, cross_count, *pieces, qt, wk, wvt),
@@ -380,25 +385,19 @@
             work,
             [
                 pltpu.VMEM((picked, width), BF),
-                pltpu.VMEM((picked, width), BF),
-                pltpu.VMEM((blocks, width, span), BF),
-                pltpu.VMEM((blocks, ONES, span), BF),
-                *rows_scratch(picked),
+                *key_scratch(picked),
             ],
         )
         parts = arrived[-1]
         (out,) = kernel_call(
             lambda *refs, n=len(parts): last_kernel(n, *refs),
             (*parts, qt, wk, wvt, acc, top, cross, features, w_out, w_up, w_down),
-            [vmem()] * (len(parts) + 6) + [hbm()] * 4,
+            [vmem()] * (len(parts) + 10),
             [sds((rows, width), BF)],
             2 * work,
             [
                 *(pltpu.VMEM(s.shape, F32) for s in state),
-                pltpu.VMEM((rows, width), BF),
-                *(pltpu.VMEM(w.shape, BF) for w in (w_out, w_up, w_down)),
-                dma((4,)),
-                *rows_scratch(rows),
+                *work_scratch(2 * half),
             ],
         )
         return out

time: 80.4 us -> 67.2 us (0.84)
  Pallas kernels: 50.8 us -> 37.9 us
    pallas_call x7, Pallas kernels: 50.8 us -> 37.9 us  [kernel_call(): pl.pallas_call(kernel, out_shape=tuple(outs), in_specs=specs, out_specs=t...]
  transfers between devices with their start and end apart: 11 -> 11, of which waited for: 2 -> 2; matrix products, arithmetic and copies ran while one was open for 1% -> 1% of each run, Pallas kernels for 50% -> 43%
where the time goes in v1:
time: 67.2 us; the launch traced here: 66.9 us
  Pallas kernels  37.9 us (56%)
  starting transfers between devices  11.5 us (17%)
  waiting for transfers between devices  10.5 us (16%)
  local copies, waits for them, and re-layouts  6.77 us (10%)
    pallas_call x7, Pallas kernels, kernel_call(): pl.pallas_call(kernel, out_shape=tuple(outs), in_specs=specs, out_specs=t...  37.9 us
    ppermute x1, waiting for transfers between devices, body(): lax.ppermute(mine, 'group', [(i, (i - 2 * k) % groups) for i in range(gro...  9.01 us
    ppermute x8, starting transfers between devices, hop(): return lax.ppermute(x, 'dom', pairs)  8.48 us
    unnamed x23, local copies, waits for them, and re-layouts  6.65 us
    ppermute x1, starting transfers between devices, body(): lax.ppermute(mine, 'group', [(i, (i - 2 * k) % groups) for i in range(gro...  3.03 us
    ppermute x8, waiting for transfers between devices, hop(): return lax.ppermute(x, 'dom', pairs)  1.48 us
  transfers between devices with their start and end apart: 11, of which 2 were waited for; matrix products, arithmetic and copies ran while one was open for 1% of the time, Pallas kernels for 43%

profile of v1, /device:TPU:0, one launch (start us, length us, event | category | flops | bytes accessed | tf_op | source)
XLA Modules:
  0.0 66.9 jit_solution(7667782389727214944)
XLA Ops:
  0.0 0.0 copy-start
  0.0 1.0 %copy-done = bf16[512,512]{1,0:T(8,128)(2,1)S(1)} copy-done((bf16[512,512]{1,0:T(8,128)(2,1)S(1)}, bf16[512,512]{1,0:T(8,128)(2,1)}, u32[]{:S(2)}) %copy-start) | copy-done | bytes 524312
  1.0 0.0 copy-start.3
  1.0 0.7 copy-done.3
  1.7 1.2 %shard_map.100.xs_ref.refs_3_ = bf16[512,512]{1,0:T(8,128)(2,1)S(1)} custom-call(s32[4]{0:T(128)S(1)} %copy-done.3, bf16[512,512]{1,0:T(8,128)(2,1)S(1)} %copy-done), custom_call_target="tpu_custom_call" | custom-call | flops 1048576 | bytes 1048592 | tf_op jit(solution)/shard_map/pallas_call | solution.py:36
  2.9 3.0 %collective-permute-start.8 = (bf16[512,512]{1,0:T(8,128)(2,1)S(1)}, bf16[512,512]{1,0:T(8,128)(2,1)S(1)}, u32[]{:S(2)}, u32[]{:S(2)}) collective-permute-start(bf16[512,512]{1,0:T(8,128)(2,1)S(1)} %shard_map.100.xs_ref.refs_3_), channel_id=1, source_target_pairs={{0,16},{8,24},{16,0},{24,8},{1,17},{9,25},{17,1},{25,9},{2,18},{10... | collective-permute-start | bytes 1572872 | tf_op jit(solution)/shard_map/ppermute | solution.py:338
  5.9 1.6 %collective-permute-start = (bf16[512,512]{1,0:T(8,128)(2,1)S(1)}, bf16[512,512]{1,0:T(8,128)(2,1)S(1)}, u32[]{:S(2)}, u32[]{:S(2)}) collective-permute-start(bf16[512,512]{1,0:T(8,128)(2,1)S(1)} %shard_map.100.xs_ref.refs_3_), channel_id=1, source_target_pairs={{0,2},{2,4},{4,6},{6,7},{7,5},{5,3},{3,1},{1,0},{8,10},{10,12},{12... | collective-permute-start | bytes 1572872 | tf_op jit(solution)/shard_map/ppermute | solution.py:326
  7.5 0.4 collective-permute-start.4
  7.9 0.0 collective-permute-start.9
  8.0 0.8 %copy.18 = s32[4,2]{1,0:T(4,128)S(1)} copy(s32[4,2]{0,1:T(2,128)} %param.18) | data formatting | bytes 64 | tf_op args[8]
  8.7 0.1 reshape.3
  8.8 9.0 %collective-permute-done.8.refs_4_ = bf16[512,512]{1,0:T(8,128)(2,1)S(1)} collective-permute-done((bf16[512,512]{1,0:T(8,128)(2,1)S(1)}, bf16[512,512]{1,0:T(8,128)(2,1)S(1)}, u32[]{:S(2)}, u32[]{:S(2)}) %collective-permute-start.8) | collective-permute-done | bytes 524320 | tf_op jit(solution)/shard_map/ppermute | solution.py:338
  17.8 0.0 collective-permute-start.10
  17.8 1.5 %collective-permute-done.refs_0_ = bf16[512,512]{1,0:T(8,128)(2,1)S(1)} collective-permute-done((bf16[512,512]{1,0:T(8,128)(2,1)S(1)}, bf16[512,512]{1,0:T(8,128)(2,1)S(1)}, u32[]{:S(2)}, u32[]{:S(2)}) %collective-permute-start) | collective-permute-done | bytes 524320 | tf_op jit(solution)/shard_map/ppermute | solution.py:326
  19.3 1.6 %collective-permute-start.1 = (bf16[512,512]{1,0:T(8,128)(2,1)S(1)}, bf16[512,512]{1,0:T(8,128)(2,1)S(1)}, u32[]{:S(2)}, u32[]{:S(2)}) collective-permute-start(bf16[512,512]{1,0:T(8,128)(2,1)S(1)} %collective-permute-done.refs_0_), channel_id=1, source_target_pairs={{0,2},{2,4},{4,6},{6,7},{7,5},{5,3},{3,1},{1,0},{8,10},{10,12},{12... | collective-permute-start | bytes 1572872 | tf_op jit(solution)/shard_map/ppermute | solution.py:326
  20.9 0.0 collective-permute-done.4.refs_1_
  20.9 0.5 collective-permute-start.5
  21.3 1.0 %copy-done.1 = bf16[512,512]{1,0:T(8,128)(2,1)S(1)} copy-done((bf16[512,512]{1,0:T(8,128)(2,1)S(1)}, bf16[512,512]{1,0:T(8,128)(2,1)}, u32[]{:S(2)}) %copy-start.1) | copy-done | bytes 524312
  22.4 0.0 copy-start.6
  22.4 1.0 %copy-done.6 = bf16[512,512]{1,0:T(8,128)(2,1)S(1)} copy-done((bf16[512,512]{1,0:T(8,128)(2,1)S(1)}, bf16[512,512]{1,0:T(8,128)(2,1)}, u32[]{:S(2)}) %copy-start.6) | copy-done | bytes 524312
  23.4 0.0 copy-start.7
  23.4 1.0 %copy-done.7 = bf16[512,512]{1,0:T(8,128)(2,1)S(1)} copy-done((bf16[512,512]{1,0:T(8,128)(2,1)S(1)}, bf16[512,512]{1,0:T(8,128)(2,1)}, u32[]{:S(2)}) %copy-start.7) | copy-done | bytes 524312
  24.5 0.0 copy-start.8
  24.5 1.0 %copy-done.8 = bf16[512,512]{1,0:T(8,128)(2,1)S(1)} copy-done((bf16[512,512]{1,0:T(8,128)(2,1)S(1)}, bf16[512,512]{1,0:T(8,128)(2,1)}, u32[]{:S(2)}) %copy-start.8) | copy-done | bytes 524312
  25.5 4.7 %shard_map.101 = (bf16[8,256,512]{2,1,0:T(8,128)(2,1)S(1)}, bf16[512,512]{1,0:T(8,128)(2,1)S(1)}, bf16[512,512]{1,0:T(8,128)(2,1)S(1)}, f32[8,80,512]{2,1,0:T(8,128)S(1)}, f32[8,512]{1,0:T(8,128)S(1)}) custom-call(bf16[512,512]{1,0:T(8,128)(2,1)S(1)} %shard_map.100.xs_ref.refs_3_, bf16[512,512]{1,0:T(8,128)(2,1)S(1)} %copy-done.1, ...), custom_call_target="tpu_custom_call" | custom-call | flops 2147483648 | bytes 7094272 | tf_op jit(solution)/shard_map/pallas_call | solution.py:36
  30.2 0.0 copy-start.10
  30.3 6.3 %shard_map.102 = (f32[8,80,512]{2,1,0:T(8,128)S(1)}, f32[8,512]{1,0:T(8,128)S(1)}) custom-call(bf16[512,512]{1,0:T(8,128)(2,1)S(1)} %collective-permute-done.refs_0_, bf16[512,512]{1,0:T(8,128)(2,1)S(1)} %collective-permute-done.4.refs_1_, bf16[8,256,512]{2,1,0:T(8,128)(2,1)S(1)} %get-tuple-element.16.refs_2_.refs_7_, ...), custom_call_target="tpu_custom_call", output_to_operand_aliasing={{0}: (5, {}), {1}: (6, {})} | custom-call | flops 4294967296 | bytes 6848512 | tf_op jit(solution)/shard_map/pallas_call | solution.py:36
  36.5 0.0 collective-permute-done.1.refs_0_
  36.5 1.6 %collective-permute-start.2 = (bf16[512,512]{1,0:T(8,128)(2,1)S(1)}, bf16[512,512]{1,0:T(8,128)(2,1)S(1)}, u32[]{:S(2)}, u32[]{:S(2)}) collective-permute-start(bf16[512,512]{1,0:T(8,128)(2,1)S(1)} %collective-permute-done.1.refs_0_), channel_id=1, source_target_pairs={{0,2},{2,4},{4,6},{6,7},{7,5},{5,3},{3,1},{1,0},{8,10},{10,12},{12... | collective-permute-start | bytes 1572872 | tf_op jit(solution)/shard_map/ppermute | solution.py:326
  38.2 0.0 collective-permute-done.5.refs_1_
  38.2 0.5 collective-permute-start.6
  38.6 0.0 collective-permute-done.9.refs_5_
  38.6 0.0 collective-permute-done.10.refs_6_
  38.6 0.0 copy-done.10
  38.6 5.3 %shard_map.105.refs_7_ = f32[512,512]{1,0:T(8,128)S(1)} custom-call(s32[8]{0:T(128)S(1)} %get-tuple-element.28.refs_0_, s32[8]{0:T(128)S(1)} %get-tuple-element.27.refs_1_, s32[4]{0:T(128)S(1)} %copy-done.10, bf16[512,512]{1,0:T(8,128)(2,1)S(1)} %shard_map.100.xs_ref.refs_3_, bf16[512,512]{1,0:T(8,128)(2,1)S(1)} %collective-permute-done.8.refs_4_, ...), custom_call_target="tpu_custom_call" | custom-call | flops 2147483648 | bytes 6291536 | tf_op jit(solution)/shard_map/pallas_call | solution.py:36
  43.9 6.3 %shard_map.103 = (f32[8,80,512]{2,1,0:T(8,128)S(1)}, f32[8,512]{1,0:T(8,128)S(1)}) custom-call(bf16[512,512]{1,0:T(8,128)(2,1)S(1)} %collective-permute-done.1.refs_0_, bf16[512,512]{1,0:T(8,128)(2,1)S(1)} %collective-permute-done.5.refs_1_, ...), custom_call_target="tpu_custom_call", output_to_operand_aliasing={{0}: (5, {}), {1}: (6, {})} | custom-call | flops 4294967296 | bytes 6848512 | tf_op jit(solution)/shard_map/pallas_call | solution.py:36
  50.2 0.0 collective-permute-done.2.refs_0_
  50.2 1.6 %collective-permute-start.3 = (bf16[256,512]{1,0:T(8,128)(2,1)S(1)}, bf16[256,512]{1,0:T(8,128)(2,1)S(1)}, u32[]{:S(2)}, u32[]{:S(2)}) collective-permute-start(bf16[256,512]{1,0:T(8,128)(2,1)S(1)} %slice.8), channel_id=1, source_target_pairs={{0,2},{2,4},{4,6},{6,7},{7,5},{5,3},{3,1},{1,0},{8,10},{10,12},{12... | collective-permute-start | bytes 786440 | tf_op jit(solution)/shard_map/ppermute | solution.py:326
  51.8 0.0 collective-permute-done.6.refs_1_
  51.9 0.7 %collective-permute-start.7 = (bf16[256,512]{1,0:T(8,128)(2,1)S(1)}, bf16[256,512]{1,0:T(8,128)(2,1)S(1)}, u32[]{:S(2)}, u32[]{:S(2)}) collective-permute-start(bf16[256,512]{1,0:T(8,128)(2,1)S(1)} %slice.9), channel_id=1, source_target_pairs={{2,0},{4,2},{6,4},{7,6},{5,7},{3,5},{1,3},{0,1},{10,8},{12,10},{14... | collective-permute-start | bytes 786440 | tf_op jit(solution)/shard_map/ppermute | solution.py:326
  52.6 6.3 %shard_map.104 = (f32[8,80,512]{2,1,0:T(8,128)S(1)}, f32[8,512]{1,0:T(8,128)S(1)}) custom-call(bf16[512,512]{1,0:T(8,128)(2,1)S(1)} %collective-permute-done.2.refs_0_, bf16[512,512]{1,0:T(8,128)(2,1)S(1)} %collective-permute-done.6.refs_1_, ...), custom_call_target="tpu_custom_call", output_to_operand_aliasing={{0}: (5, {}), {1}: (6, {})} | custom-call | flops 4294967296 | bytes 6848512 | tf_op jit(solution)/shard_map/pallas_call | solution.py:36
  58.9 0.0 collective-permute-done.3.refs_0_
  58.9 0.0 collective-permute-done.7.refs_1_
  58.9 0.0 copy-done.2
  58.9 0.0 copy-done.4
  58.9 0.0 copy-done.5
  58.9 0.0 copy-done.9
  59.0 7.9 %shard_map.106 = bf16[512,512]{1,0:T(8,128)(2,1)} custom-call(bf16[256,512]{1,0:T(8,128)(2,1)S(1)} %collective-permute-done.3.refs_0_, bf16[256,512]{1,0:T(8,128)(2,1)S(1)} %collective-permute-done.7.refs_1_, bf16[8,256,512]{2,1,0:T(8,128)(2,1)S(1)} %get-tuple-element.16.refs_2_.refs_7_, bf16[512,512]{1,0:T(8,128)(2,1)S(1)} %get-tuple-element.17.refs_3_.refs_8_, ...), custom_call_target="tpu_custom_call" | custom-call | flops 4294967296 | bytes 11812864 | tf_op jit(solution)/shard_map/pallas_call | solution.py:36
  (8 shorter events, 0.1 us)
Async XLA Ops:
  0.0 1.0 %copy-start = (bf16[512,512]{1,0:T(8,128)(2,1)S(1)}, bf16[512,512]{1,0:T(8,128)(2,1)}, u32[]{:S(2)}) copy-start(bf16[512,512]{1,0:T(8,128)(2,1)} %refs_8_.1) | copy-start | bytes 1572868
  1.0 0.7 copy-start.3
  2.9 15.0 %collective-permute-start.8 = (bf16[512,512]{1,0:T(8,128)(2,1)S(1)}, bf16[512,512]{1,0:T(8,128)(2,1)S(1)}, u32[]{:S(2)}, u32[]{:S(2)}) collective-permute-start(bf16[512,512]{1,0:T(8,128)(2,1)S(1)} %shard_map.100.xs_ref.refs_3_), channel_id=1, source_target_pairs={{0,16},{8,24},{16,0},{24,8},{1,17},{9,25},{17,1},{25,9},{2,18},{10... | collective-permute-start | bytes 1572872 | tf_op jit(solution)/shard_map/ppermute | solution.py:338
  5.9 13.4 %collective-permute-start = (bf16[512,512]{1,0:T(8,128)(2,1)S(1)}, bf16[512,512]{1,0:T(8,128)(2,1)S(1)}, u32[]{:S(2)}, u32[]{:S(2)}) collective-permute-start(bf16[512,512]{1,0:T(8,128)(2,1)S(1)} %shard_map.100.xs_ref.refs_3_), channel_id=1, source_target_pairs={{0,2},{2,4},{4,6},{6,7},{7,5},{5,3},{3,1},{1,0},{8,10},{10,12},{12... | collective-permute-start | bytes 1572872 | tf_op jit(solution)/shard_map/ppermute | solution.py:326
  7.5 13.4 %collective-permute-start.4 = (bf16[512,512]{1,0:T(8,128)(2,1)S(1)}, bf16[512,512]{1,0:T(8,128)(2,1)S(1)}, u32[]{:S(2)}, u32[]{:S(2)}) collective-permute-start(bf16[512,512]{1,0:T(8,128)(2,1)S(1)} %shard_map.100.xs_ref.refs_3_), channel_id=1, source_target_pairs={{2,0},{4,2},{6,4},{7,6},{5,7},{3,5},{1,3},{0,1},{10,8},{12,10},{14... | collective-permute-start | bytes 1572872 | tf_op jit(solution)/shard_map/ppermute | solution.py:326
  7.9 30.7 %collective-permute-start.9 = (bf16[512,512]{1,0:T(8,128)(2,1)S(1)}, bf16[512,512]{1,0:T(8,128)(2,1)S(1)}, u32[]{:S(2)}, u32[]{:S(2)}) collective-permute-start(bf16[512,512]{1,0:T(8,128)(2,1)S(1)} %shard_map.100.xs_ref.refs_3_), channel_id=1, source_target_pairs={{0,8},{8,0},{16,24},{24,16},{1,9},{9,1},{17,25},{25,17},{2,10},{10... | collective-permute-start | bytes 1572872 | tf_op jit(solution)/shard_map/ppermute | solution.py:342
  17.8 20.8 %collective-permute-start.10 = (bf16[512,512]{1,0:T(8,128)(2,1)S(1)}, bf16[512,512]{1,0:T(8,128)(2,1)S(1)}, u32[]{:S(2)}, u32[]{:S(2)}) collective-permute-start(bf16[512,512]{1,0:T(8,128)(2,1)S(1)} %collective-permute-done.8.refs_4_), channel_id=1, source_target_pairs={{0,8},{8,0},{16,24},{24,16},{1,9},{9,1},{17,25},{25,17},{2,10},{10... | collective-permute-start | bytes 1572872 | tf_op jit(solution)/shard_map/ppermute | solution.py:342
  19.3 17.2 %collective-permute-start.1 = (bf16[512,512]{1,0:T(8,128)(2,1)S(1)}, bf16[512,512]{1,0:T(8,128)(2,1)S(1)}, u32[]{:S(2)}, u32[]{:S(2)}) collective-permute-start(bf16[512,512]{1,0:T(8,128)(2,1)S(1)} %collective-permute-done.refs_0_), channel_id=1, source_target_pairs={{0,2},{2,4},{4,6},{6,7},{7,5},{5,3},{3,1},{1,0},{8,10},{10,12},{12... | collective-permute-start | bytes 1572872 | tf_op jit(solution)/shard_map/ppermute | solution.py:326
  20.9 17.3 %collective-permute-start.5 = (bf16[512,512]{1,0:T(8,128)(2,1)S(1)}, bf16[512,512]{1,0:T(8,128)(2,1)S(1)}, u32[]{:S(2)}, u32[]{:S(2)}) collective-permute-start(bf16[512,512]{1,0:T(8,128)(2,1)S(1)} %collective-permute-done.4.refs_1_), channel_id=1, source_target_pairs={{2,0},{4,2},{6,4},{7,6},{5,7},{3,5},{1,3},{0,1},{10,8},{12,10},{14... | collective-permute-start | bytes 1572872 | tf_op jit(solution)/shard_map/ppermute | solution.py:326
  21.3 1.0 %copy-start.1 = (bf16[512,512]{1,0:T(8,128)(2,1)S(1)}, bf16[512,512]{1,0:T(8,128)(2,1)}, u32[]{:S(2)}) copy-start(bf16[512,512]{1,0:T(8,128)(2,1)} %refs_8_.1) | copy-start | bytes 1572868
  22.4 1.0 %copy-start.6 = (bf16[512,512]{1,0:T(8,128)(2,1)S(1)}, bf16[512,512]{1,0:T(8,128)(2,1)}, u32[]{:S(2)}) copy-start(bf16[512,512]{1,0:T(8,128)(2,1)} %wq_hbm.1) | copy-start | bytes 1572868
  23.4 1.0 %copy-start.7 = (bf16[512,512]{1,0:T(8,128)(2,1)S(1)}, bf16[512,512]{1,0:T(8,128)(2,1)}, u32[]{:S(2)}) copy-start(bf16[512,512]{1,0:T(8,128)(2,1)} %wk_hbm.1) | copy-start | bytes 1572868
  24.5 1.0 %copy-start.8 = (bf16[512,512]{1,0:T(8,128)(2,1)S(1)}, bf16[512,512]{1,0:T(8,128)(2,1)}, u32[]{:S(2)}) copy-start(bf16[512,512]{1,0:T(8,128)(2,1)} %wv_hbm.1) | copy-start | bytes 1572868
  30.2 8.4 %copy-start.10 = (s32[4]{0:T(128)S(1)}, s32[4]{0:T(128)}, u32[]{:S(2)}) copy-start(s32[4]{0:T(128)} %refs_2_.1) | copy-start | bytes 52
  36.5 13.7 %collective-permute-start.2 = (bf16[512,512]{1,0:T(8,128)(2,1)S(1)}, bf16[512,512]{1,0:T(8,128)(2,1)S(1)}, u32[]{:S(2)}, u32[]{:S(2)}) collective-permute-start(bf16[512,512]{1,0:T(8,128)(2,1)S(1)} %collective-permute-done.1.refs_0_), channel_id=1, source_target_pairs={{0,2},{2,4},{4,6},{6,7},{7,5},{5,3},{3,1},{1,0},{8,10},{10,12},{12... | collective-permute-start | bytes 1572872 | tf_op jit(solution)/shard_map/ppermute | solution.py:326
  38.2 13.7 %collective-permute-start.6 = (bf16[512,512]{1,0:T(8,128)(2,1)S(1)}, bf16[512,512]{1,0:T(8,128)(2,1)S(1)}, u32[]{:S(2)}, u32[]{:S(2)}) collective-permute-start(bf16[512,512]{1,0:T(8,128)(2,1)S(1)} %collective-permute-done.5.refs_1_), channel_id=1, source_target_pairs={{2,0},{4,2},{6,4},{7,6},{5,7},{3,5},{1,3},{0,1},{10,8},{12,10},{14... | collective-permute-start | bytes 1572872 | tf_op jit(solution)/shard_map/ppermute | solution.py:326
  50.2 8.7 %collective-permute-start.3 = (bf16[256,512]{1,0:T(8,128)(2,1)S(1)}, bf16[256,512]{1,0:T(8,128)(2,1)S(1)}, u32[]{:S(2)}, u32[]{:S(2)}) collective-permute-start(bf16[256,512]{1,0:T(8,128)(2,1)S(1)} %slice.8), channel_id=1, source_target_pairs={{0,2},{2,4},{4,6},{6,7},{7,5},{5,3},{3,1},{1,0},{8,10},{10,12},{12... | collective-permute-start | bytes 786440 | tf_op jit(solution)/shard_map/ppermute | solution.py:326
  51.9 7.0 %collective-permute-start.7 = (bf16[256,512]{1,0:T(8,128)(2,1)S(1)}, bf16[256,512]{1,0:T(8,128)(2,1)S(1)}, u32[]{:S(2)}, u32[]{:S(2)}) collective-permute-start(bf16[256,512]{1,0:T(8,128)(2,1)S(1)} %slice.9), channel_id=1, source_target_pairs={{2,0},{4,2},{6,4},{7,6},{5,7},{3,5},{1,3},{0,1},{10,8},{12,10},{14... | collective-permute-start | bytes 786440 | tf_op jit(solution)/shard_map/ppermute | solution.py:326
  52.6 6.3 %copy-start.2 = (bf16[512,512]{1,0:T(8,128)(2,1)S(1)}, bf16[512,512]{1,0:T(8,128)(2,1)}, u32[]{:S(2)}) copy-start(bf16[512,512]{1,0:T(8,128)(2,1)} %refs_8_.1) | copy-start | bytes 1572868
  52.6 6.3 %copy-start.4 = (bf16[512,2048]{1,0:T(8,128)(2,1)S(1)}, bf16[512,2048]{1,0:T(8,128)(2,1)}, u32[]{:S(2)}) copy-start(bf16[512,2048]{1,0:T(8,128)(2,1)} %refs_10_.1) | copy-start | bytes 6291460
  52.6 6.3 %copy-start.5 = (bf16[2048,512]{1,0:T(8,128)(2,1)S(1)}, bf16[2048,512]{1,0:T(8,128)(2,1)}, u32[]{:S(2)}) copy-start(bf16[2048,512]{1,0:T(8,128)(2,1)} %refs_11_.1) | copy-start | bytes 6291460
  52.6 6.3 %copy-start.9 = (bf16[512,512]{1,0:T(8,128)(2,1)S(1)}, bf16[512,512]{1,0:T(8,128)(2,1)}, u32[]{:S(2)}) copy-start(bf16[512,512]{1,0:T(8,128)(2,1)} %refs_9_.1) | copy-start | bytes 1572868
